TPU v7x, 512 devices: a whole 4x4x16 slice. The times are simulated.
512 devices in a mesh: seq: 16 (over y, x), mp: 32 (over z, core).
Axes of the slice: x: 4, y: 4, z: 16, core: 2. Of those that a mesh axis runs over, the one named last changes fastest.
Arguments:
- q_proj: bfloat16 [4096, 8192], P('seq', 'mp'), may hold values from -6 to 6
- k_proj: bfloat16 [4096, 8192], P('seq', 'mp'), may hold values from -6 to 6
- v_proj: bfloat16 [4096, 8192], P('seq', 'mp'), may hold values from -6 to 6
- out_grad: bfloat16 [4096, 8192], P('seq', 'mp'), may hold values from -0.75 to 0.75
- out_weight: bfloat16 [8192, 8192], P('mp', 'seq'), may hold values from -0.0625 to 0.0625
- taps: float32 [7, 512], P(None, 'mp'), may hold values from -2.4 to 2.4
Outputs:
- grad_q: bfloat16 [4096, 8192], P('seq', 'mp')
- grad_k: bfloat16 [4096, 8192], P('seq', 'mp')
- grad_v: bfloat16 [4096, 8192], P('seq', 'mp')
- grad_weight: float32 [8192, 8192], P('mp', 'seq')
- grad_taps: float32 [7, 512], P(None, 'mp')
All inputs are finite; a program needn't handle non-finite values.
Results may differ from a plain program's by a relative error of at most 0.0029.
Values may be sent and summed in bfloat16 or wider, within the bound.
A program may use at most 64 MiB of HBM per device.

v0:
```python
import jax
import jax.numpy as jnp
from jax import lax
from jax.sharding import PartitionSpec as P

TAPS = 7
GROUP = 16


def passed_along(array, axis, by):
    count = lax.axis_size(axis)
    pairs = [(i, i + by) for i in range(count) if 0 <= i + by < count]
    return lax.ppermute(array, axis, pairs)


def shards(q_proj, k_proj, v_proj, out_grad, out_weight, taps):
    tokens, channels = q_proj.shape
    rim_rows = TAPS - 1
    q_full = q_proj.astype(jnp.float32)
    k_full = k_proj.astype(jnp.float32)
    v_full = v_proj.astype(jnp.float32)
    spread = jnp.broadcast_to(taps[:, :, None], (TAPS, taps.shape[1], GROUP)).reshape(
        TAPS, channels
    )
    tail_rows = jnp.stack([k_proj[tokens - rim_rows :], v_proj[tokens - rim_rows :]])
    before = passed_along(tail_rows, "seq", 1)
    keys_wide = jnp.concatenate([before[0], k_proj], 0).astype(jnp.float32)
    values_wide = jnp.concatenate([before[1], v_proj], 0).astype(jnp.float32)
    product = keys_wide * values_wide
    filtered = jnp.zeros((tokens, channels), jnp.float32)
    for offset in range(TAPS):
        filtered = (
            filtered + spread[offset] * product[rim_rows - offset : rim_rows - offset + tokens]
        )
    gated = (q_full * filtered).astype(jnp.bfloat16)
    seq_count, mp_count = (lax.axis_size("seq"), lax.axis_size("mp"))
    cores = mp_count // seq_count
    pairs = [
        (t * mp_count + cores * z + c, z * mp_count + cores * t + c)
        for t in range(seq_count)
        for z in range(seq_count)
        for c in range(cores)
    ]
    crossed = lax.ppermute(out_grad, ("seq", "mp"), pairs)
    tiles = lax.all_gather(crossed, "mp", axis=0)
    columns = (
        tiles.reshape(seq_count, cores, tokens, channels)
        .transpose(0, 2, 1, 3)
        .reshape(seq_count * tokens, cores * channels)
    )
    partial = lax.dot_general(
        columns, out_weight, (((1,), (1,)), ((), ())), preferred_element_type=jnp.float32
    )
    grad_gated = lax.psum_scatter(partial, "seq", scatter_dimension=0, tiled=True)
    grad_weight = lax.dot_general(
        lax.all_gather(gated, "seq", axis=0, tiled=True),
        columns,
        (((0,), (0,)), ((), ())),
        preferred_element_type=jnp.float32,
    )
    grad_q = (grad_gated * filtered).astype(jnp.bfloat16)
    grad_filtered = grad_gated * q_full
    following = passed_along(grad_filtered[:rim_rows], "seq", -1)
    grad_ext = jnp.concatenate([grad_filtered, following], 0)
    grad_product = jnp.zeros((tokens, channels), jnp.float32)
    for offset in range(TAPS):
        grad_product = grad_product + spread[offset] * grad_ext[offset : offset + tokens]
    grad_k = (grad_product * v_full).astype(jnp.bfloat16)
    grad_v = (grad_product * k_full).astype(jnp.bfloat16)
    filter_terms = jnp.stack(
        [
            jnp.sum(grad_filtered * product[rim_rows - offset : rim_rows - offset + tokens], 0)
            for offset in range(TAPS)
        ]
    )
    filter_local = filter_terms.reshape(TAPS, channels // GROUP, GROUP).sum(-1)
    grad_taps = lax.psum(filter_local, "seq")
    return (grad_q, grad_k, grad_v, grad_weight, grad_taps)


def solution(mesh):
    placed = (
        P("seq", "mp"),
        P("seq", "mp"),
        P("seq", "mp"),
        P("seq", "mp"),
        P("mp", "seq"),
        P(None, "mp"),
    )
    return jax.shard_map(
        shards,
        mesh=mesh,
        in_specs=placed,
        out_specs=(P("seq", "mp"), P("seq", "mp"), P("seq", "mp"), P("mp", "seq"), P(None, "mp")),
        check_vma=False,
    )
```

profile of v0, /device:TPU:32, one launch (start us, length us, event | category | flops | bytes accessed | tf_op | source)
XLA Modules:
  0.0 327.7 jit_solution(6569584320959466278)
XLA Ops:
  7.2 0.0 all-gather.6.cloned.1.call-start
  7.2 3.1 collective-permute-start
  10.3 12.5 %collective-permute-done = bf16[256,256]{1,0:T(8,128)(2,1)S(1)} collective-permute-done((bf16[256,256]{1,0:T(8,128)(2,1)}, bf16[256,256]{1,0:T(8,128)(2,1)S(1)}, u32[]{:S(2)}, u32[]{:S(2)}) %collective-permute-start) | collective-permute-done | bytes 131104 | tf_op jit(solution)/shard_map/ppermute | solution.py:44
  22.8 0.7 copy-done.5
  23.5 0.0 all-gather.6.cloned.1.call-update
  23.5 0.0 all-gather.4.cloned.1.call-start
  23.5 0.7 slice_bitcast_fusion.2
  24.3 1.3 collective-permute-start.1
  25.6 0.9 slice_bitcast_fusion.10
  26.5 0.1 broadcast_in_dim.44
  26.6 0.1 broadcast_in_dim.45
  26.7 0.1 broadcast_in_dim.42
  26.8 0.1 broadcast_in_dim.43
  26.8 0.1 broadcast_in_dim.40
  26.9 0.1 broadcast_in_dim.41
  27.0 0.1 broadcast_in_dim.38
  27.1 0.1 broadcast_in_dim.39
  27.1 0.1 broadcast_in_dim.36
  27.2 0.1 broadcast_in_dim.37
  27.3 0.1 broadcast_in_dim.34
  27.4 0.1 broadcast_in_dim.35
  27.4 0.1 broadcast_in_dim.32
  27.5 0.1 broadcast_in_dim.33
  27.6 0.0 collective-permute-done.1
  27.6 1.0 convert_multiply_fusion.2
  28.7 1.8 fusion
  30.5 0.0 reduce-scatter.2.cloned.1.call-start
  30.6 87.3 %all-gather.6.cloned.1.call-done = bf16[8192,256]{1,0:T(8,128)(2,1)} async-done(((bf16[256,256]{1,0:T(8,128)(2,1)}), bf16[8192,256]{1,0:T(8,128)(2,1)}) %all-gather.6.cloned.1.call-update) | async-done | bytes 4194320 | tf_op jit(solution)/shard_map/all_gather | solution.py:45
  117.8 8.0 %copy.12 = bf16[16,2,256,256]{2,0,3,1:T(8,128)(2,1)} copy(bf16[16,2,256,256]{3,2,1,0:T(8,128)(2,1)} %bitcast.36) | data formatting | bytes 8388608 | tf_op jit(solution)/shard_map/reshape | solution.py:47
  125.8 4.4 %copy.13 = bf16[64,8,16,256]{3,1,2,0:T(8,128)(2,1)S(1)} copy(bf16[64,8,16,256]{3,2,1,0:T(8,128)(2,1)} %bitcast.35) | data formatting | bytes 8388608
  130.2 2.0 copy-done.1
  132.2 3.2 fusion.19
  135.5 43.0 %all-gather.4.cloned.1.call-done = bf16[4096,256]{1,0:T(8,128)(2,1)} async-done(((bf16[256,256]{1,0:T(8,128)(2,1)}), bf16[4096,256]{1,0:T(8,128)(2,1)}) %all-gather.4.cloned.1.call-update) | async-done | bytes 2097168 | tf_op jit(solution)/shard_map/all_gather | solution.py:56
  178.5 4.9 %fusion.20 = f32[256,512]{1,0:T(8,128)} fusion(bf16[4096,256]{1,0:T(8,128)(2,1)} %all-gather.4.cloned.1.call-done, bf16[4096,512]{0,1:T(8,128)(2,1)} %bitcast.34), kind=kOutput, calls=%fused_computation.61 | convolution fusion | flops 1073741824 | bytes 6815744 | tf_op jit(solution)/shard_map/dot_general | solution.py:55
  183.4 91.8 %reduce-scatter.2.cloned.1.call-done = f32[256,256]{1,0:T(8,128)} async-done(((f32[4096,256]{1,0:T(8,128)}), f32[256,256]{1,0:T(8,128)}) %reduce-scatter.2.cloned.1.call-update) | async-done | bytes 262160 | tf_op jit(solution)/shard_map/reduce_scatter | solution.py:54
  275.2 1.9 multiply_reduce_fusion
  277.1 1.3 collective-permute-start.2
  278.4 0.1 stack.36
  278.4 0.1 stack.37
  278.5 0.1 stack.38
  278.6 0.1 stack.39
  278.7 0.1 stack.40
  278.8 0.1 stack.41
  278.8 0.1 stack.42
  279.0 0.1 reduce_sum.79
  279.1 40.5 %psum.7 = f32[7,16]{1,0:T(8,128)} all-reduce(f32[7,16]{1,0:T(8,128)S(1)} %reduce_sum.79), channel_id=1, replica_groups=mesh['seq'=16,'mp'=32] {'seq'}, use_global_device_ids=true, to_apply=%region_9.0 | all-reduce | flops 112 | bytes 896 | tf_op jit(solution)/shard_map/psum | solution.py:77
  319.6 0.9 multiply_convert_fusion
  320.5 0.7 multiply_convert_fusion.1
  (23 shorter events, 0.1 us)
Async XLA Ops:
  7.2 125.0 %copy-start = (bf16[256,512]{1,0:T(8,128)(2,1)S(1)}, bf16[256,512]{1,0:T(8,128)(2,1)}, u32[]{:S(2)}) copy-start(bf16[256,512]{1,0:T(8,128)(2,1)} %param.10) | copy-start | bytes 786436
  7.2 110.7 %all-gather.6.cloned.1.call-start = ((), (), s32[]{:S(2)}) async-start(), calls=%async_computation.3 | async-start | bytes 4325376 | tf_op jit(solution)/shard_map/all_gather | solution.py:45
  7.2 15.6 %collective-permute-start = (bf16[256,256]{1,0:T(8,128)(2,1)}, bf16[256,256]{1,0:T(8,128)(2,1)S(1)}, u32[]{:S(2)}, u32[]{:S(2)}) collective-permute-start(bf16[256,256]{1,0:T(8,128)(2,1)} %param.9), channel_id=1, source_target_pairs={{0,0},{1,1},{2,32},{3,33},{4,64},{5,65},{6,96},{7,97},{8,128},{9,1... | collective-permute-start | bytes 393224 | tf_op jit(solution)/shard_map/ppermute | solution.py:44
  22.8 0.7 copy-start.5
  23.5 155.0 %all-gather.4.cloned.1.call-start = ((), (), s32[]{:S(2)}) async-start(), calls=%async_computation.2 | async-start | bytes 2228224 | tf_op jit(solution)/shard_map/all_gather | solution.py:56
  24.3 3.3 %collective-permute-start.1 = (bf16[2,6,256]{2,1,0:T(8,128)(2,1)S(1)}, bf16[2,6,256]{2,1,0:T(8,128)(2,1)S(1)}, u32[]{:S(2)}, u32[]{:S(2)}) collective-permute-start(bf16[2,6,256]{2,1,0:T(8,128)(2,1)S(1)} %pad_maximum_fusion.1), channel_id=1, source_target_pairs={{0,32},{32,64},{64,96},{96,128},{128,160},{160,192},{192,224},{224... | collective-permute-start | bytes 18440 | tf_op jit(solution)/shard_map/ppermute | solution.py:13
  30.5 244.7 %reduce-scatter.2.cloned.1.call-start = ((), (), s32[]{:S(2)}) async-start(), calls=%async_computation.1 | async-start | bytes 4456448 | tf_op jit(solution)/shard_map/reduce_scatter | solution.py:54
  130.2 2.0 copy-start.1
  135.4 139.8 %copy-start.4 = (bf16[256,256]{1,0:T(8,128)(2,1)S(1)}, bf16[256,256]{1,0:T(8,128)(2,1)}, u32[]{:S(2)}) copy-start(bf16[256,256]{1,0:T(8,128)(2,1)} %param.6) | copy-start | bytes 393220
  135.4 184.1 %copy-start.2 = (bf16[256,256]{1,0:T(8,128)(2,1)S(1)}, bf16[256,256]{1,0:T(8,128)(2,1)}, u32[]{:S(2)}) copy-start(bf16[256,256]{1,0:T(8,128)(2,1)} %param.7) | copy-start | bytes 393220
  135.4 185.0 %copy-start.3 = (bf16[256,256]{1,0:T(8,128)(2,1)S(1)}, bf16[256,256]{1,0:T(8,128)(2,1)}, u32[]{:S(2)}) copy-start(bf16[256,256]{1,0:T(8,128)(2,1)} %param.8) | copy-start | bytes 393220
  277.1 42.5 %collective-permute-start.2 = (f32[6,256]{1,0:T(8,128)S(1)}, f32[6,256]{1,0:T(8,128)S(1)}, u32[]{:S(2)}, u32[]{:S(2)}) collective-permute-start(f32[6,256]{1,0:T(8,128)S(1)} %slice.158), channel_id=1, source_target_pairs={{32,0},{64,32},{96,64},{128,96},{160,128},{192,160},{224,192},{256... | collective-permute-start | bytes 18440 | tf_op jit(solution)/shard_map/ppermute | solution.py:13
Sparse Core Ops, SparseCore 0:
  23.6 94.1 all-gather.5
  121.4 57.0 all-gather.3
  182.7 92.4 reduce-scatter.1
where the time goes:
time: 328 us
  waiting for transfers between devices  235 us (72%)
  blocking collectives  40.5 us (12%)
  local copies, waits for them, and re-layouts  18.3 us (6%)
  between operations  13.9 us (4%)
  matrix products  8.15 us (2%)
  other arithmetic  6.39 us (2%)
  starting transfers between devices  5.76 us (2%)
    reduce_scatter x1, waiting for transfers between devices, shards(): lax.psum_scatter(partial, 'seq', scatter_dimension=0, tiled=True)  91.8 us
    all_gather x1, waiting for transfers between devices, shards(): tiles = lax.all_gather(crossed, 'mp', axis=0)  87.3 us
    all_gather x1, waiting for transfers between devices, shards(): lax.all_gather(gated, 'seq', axis=0, tiled=True)  43 us
    psum x1, blocking collectives, shards(): grad_taps = lax.psum(filter_local, 'seq')  40.5 us
    ppermute x1, waiting for transfers between devices, shards(): crossed = lax.ppermute(out_grad, ('seq', 'mp'), pairs)  12.5 us
    reshape x1, local copies, waits for them, and re-layouts, shards(): tiles.reshape(seq_count, cores, tokens, channels).transpose(0, 2, 1, 3)  7.96 us
    unnamed x19, local copies, waits for them, and re-layouts  7.08 us
  transfers between devices with their start and end apart: 6, of which 4 were waited for; matrix products, arithmetic and copies ran while one was open for 8% of the time, Pallas kernels for 0%

commit v1 on v0

--- a/solution.py
+++ b/solution.py
@@ -74,7 +74,7 @@
         ]
     )
     filter_local = filter_terms.reshape(TAPS, channels // GROUP, GROUP).sum(-1)
-    grad_taps = lax.psum(filter_local, "seq")
+    grad_taps = jnp.sum(lax.all_gather(filter_local, "seq"), axis=0)
     return (grad_q, grad_k, grad_v, grad_weight, grad_taps)
 
 

time: 328 us -> 313 us (0.954)
  blocking collectives: 40.5 us -> 25 us
    psum x1 -> x0, blocking collectives: 40.5 us -> none  [shards(): grad_taps = lax.psum(filter_local, 'seq')]
    all_gather x0 -> x1, blocking collectives: none -> 25 us  [shards(): grad_taps = jnp.sum(lax.all_gather(filter_local, 'seq'), axis=0)]
  transfers between devices with their start and end apart: 6 -> 6, of which waited for: 4 -> 4; matrix products, arithmetic and copies ran while one was open for 8% -> 9% of each run, Pallas kernels for 0% -> 0%
where the time goes in v1:
time: 313 us
  waiting for transfers between devices  235 us (75%)
  blocking collectives  25 us (8%)
  local copies, waits for them, and re-layouts  18.3 us (6%)
  between operations  13.9 us (4%)
  matrix products  8.16 us (3%)
  other arithmetic  7.01 us (2%)
  starting transfers between devices  5.76 us (2%)
    reduce_scatter x1, waiting for transfers between devices, shards(): lax.psum_scatter(partial, 'seq', scatter_dimension=0, tiled=True)  91.8 us
    all_gather x1, waiting for transfers between devices, shards(): tiles = lax.all_gather(crossed, 'mp', axis=0)  87.3 us
    all_gather x1, waiting for transfers between devices, shards(): lax.all_gather(gated, 'seq', axis=0, tiled=True)  43 us
    all_gather x1, blocking collectives, shards(): grad_taps = jnp.sum(lax.all_gather(filter_local, 'seq'), axis=0)  25 us
    ppermute x1, waiting for transfers between devices, shards(): crossed = lax.ppermute(out_grad, ('seq', 'mp'), pairs)  12.5 us
    reshape x1, local copies, waits for them, and re-layouts, shards(): tiles.reshape(seq_count, cores, tokens, channels).transpose(0, 2, 1, 3)  7.96 us
    unnamed x19, local copies, waits for them, and re-layouts  7.08 us
  transfers between devices with their start and end apart: 6, of which 4 were waited for; matrix products, arithmetic and copies ran while one was open for 9% of the time, Pallas kernels for 0%

profile of v1, /device:TPU:32, one launch (start us, length us, event | category | flops | bytes accessed | tf_op | source)
XLA Modules:
  0.0 312.9 jit_solution(5977201514872526966)
XLA Ops:
  7.2 0.0 all-gather.8.cloned.1.call-start
  7.2 3.1 collective-permute-start
  10.3 12.5 %collective-permute-done = bf16[256,256]{1,0:T(8,128)(2,1)S(1)} collective-permute-done((bf16[256,256]{1,0:T(8,128)(2,1)}, bf16[256,256]{1,0:T(8,128)(2,1)S(1)}, u32[]{:S(2)}, u32[]{:S(2)}) %collective-permute-start) | collective-permute-done | bytes 131104 | tf_op jit(solution)/shard_map/ppermute | solution.py:44
  22.8 0.7 copy-done.5
  23.5 0.0 all-gather.6.cloned.1.call-start
  23.5 0.7 slice_bitcast_fusion.2
  24.3 1.3 collective-permute-start.1
  25.6 0.9 slice_bitcast_fusion.10
  26.5 0.1 broadcast_in_dim.44
  26.6 0.1 broadcast_in_dim.45
  26.7 0.1 broadcast_in_dim.42
  26.8 0.1 broadcast_in_dim.43
  26.8 0.1 broadcast_in_dim.40
  26.9 0.1 broadcast_in_dim.41
  27.0 0.1 broadcast_in_dim.38
  27.1 0.1 broadcast_in_dim.39
  27.1 0.1 broadcast_in_dim.36
  27.2 0.1 broadcast_in_dim.37
  27.3 0.1 broadcast_in_dim.34
  27.4 0.1 broadcast_in_dim.35
  27.4 0.1 broadcast_in_dim.32
  27.5 0.1 broadcast_in_dim.33
  27.6 0.0 collective-permute-done.1
  27.6 1.0 convert_multiply_fusion.2
  28.7 1.8 fusion
  30.5 0.0 reduce-scatter.2.cloned.1.call-start
  30.6 87.3 %all-gather.8.cloned.1.call-done = bf16[8192,256]{1,0:T(8,128)(2,1)} async-done(((bf16[256,256]{1,0:T(8,128)(2,1)}), bf16[8192,256]{1,0:T(8,128)(2,1)}) %all-gather.8.cloned.1.call-update) | async-done | bytes 4194320 | tf_op jit(solution)/shard_map/all_gather | solution.py:45
  117.8 8.0 %copy.13 = bf16[16,2,256,256]{2,0,3,1:T(8,128)(2,1)} copy(bf16[16,2,256,256]{3,2,1,0:T(8,128)(2,1)} %bitcast.37) | data formatting | bytes 8388608 | tf_op jit(solution)/shard_map/reshape | solution.py:47
  125.8 4.4 %copy.14 = bf16[64,8,16,256]{3,1,2,0:T(8,128)(2,1)S(1)} copy(bf16[64,8,16,256]{3,2,1,0:T(8,128)(2,1)} %bitcast.36) | data formatting | bytes 8388608
  130.2 2.0 copy-done.1
  132.2 3.2 %fusion.19 = f32[4096,256]{1,0:T(8,128)} fusion(bf16[4096,512]{0,1:T(8,128)(2,1)S(1)} %bitcast.34, bf16[256,512]{1,0:T(8,128)(2,1)S(1)} %copy-done), kind=kOutput, calls=%fused_computation.60 | convolution fusion | flops 1073741824 | bytes 8650752 | tf_op jit(solution)/shard_map/dot_general | solution.py:51
  135.5 43.0 %all-gather.6.cloned.1.call-done = bf16[4096,256]{1,0:T(8,128)(2,1)} async-done(((bf16[256,256]{1,0:T(8,128)(2,1)}), bf16[4096,256]{1,0:T(8,128)(2,1)}) %all-gather.6.cloned.1.call-update) | async-done | bytes 2097168 | tf_op jit(solution)/shard_map/all_gather | solution.py:56
  178.5 4.9 %fusion.20 = f32[256,512]{1,0:T(8,128)} fusion(bf16[4096,256]{1,0:T(8,128)(2,1)} %all-gather.6.cloned.1.call-done, bf16[4096,512]{0,1:T(8,128)(2,1)} %bitcast.35), kind=kOutput, calls=%fused_computation.61 | convolution fusion | flops 1073741824 | bytes 6815744 | tf_op jit(solution)/shard_map/dot_general | solution.py:55
  183.4 91.8 %reduce-scatter.2.cloned.1.call-done = f32[256,256]{1,0:T(8,128)} async-done(((f32[4096,256]{1,0:T(8,128)}), f32[256,256]{1,0:T(8,128)}) %reduce-scatter.2.cloned.1.call-update) | async-done | bytes 262160 | tf_op jit(solution)/shard_map/reduce_scatter | solution.py:54
  275.2 1.9 multiply_reduce_fusion
  277.1 1.3 collective-permute-start.2
  278.4 0.1 stack.36
  278.4 0.1 stack.37
  278.5 0.1 stack.38
  278.6 0.1 stack.39
  278.7 0.1 stack.40
  278.8 0.1 stack.41
  278.8 0.1 stack.42
  279.0 0.1 reduce_sum.88
  279.1 25.0 %all-gather.2 = f32[16,7,16]{2,1,0:T(8,128)S(1)} all-gather(f32[1,7,16]{2,1,0:T(8,128)S(1)} %bitcast.38), channel_id=3, replica_groups=mesh['seq'=16,'mp'=32] {'seq'}, dimensions={0}, use_global_device_ids=true | all-gather | bytes 7616 | tf_op jit(solution)/shard_map/all_gather | solution.py:77
  304.1 0.6 reduce_sum.89
  304.7 0.9 multiply_convert_fusion
  305.6 0.7 multiply_convert_fusion.1
  (24 shorter events, 0.1 us)
Async XLA Ops:
  7.2 125.0 %copy-start = (bf16[256,512]{1,0:T(8,128)(2,1)S(1)}, bf16[256,512]{1,0:T(8,128)(2,1)}, u32[]{:S(2)}) copy-start(bf16[256,512]{1,0:T(8,128)(2,1)} %param.10) | copy-start | bytes 786436
  7.2 110.7 %all-gather.8.cloned.1.call-start = ((), (), s32[]{:S(2)}) async-start(), calls=%async_computation.3 | async-start | bytes 4325376 | tf_op jit(solution)/shard_map/all_gather | solution.py:45
  7.2 15.6 %collective-permute-start = (bf16[256,256]{1,0:T(8,128)(2,1)}, bf16[256,256]{1,0:T(8,128)(2,1)S(1)}, u32[]{:S(2)}, u32[]{:S(2)}) collective-permute-start(bf16[256,256]{1,0:T(8,128)(2,1)} %param.9), channel_id=1, source_target_pairs={{0,0},{1,1},{2,32},{3,33},{4,64},{5,65},{6,96},{7,97},{8,128},{9,1... | collective-permute-start | bytes 393224 | tf_op jit(solution)/shard_map/ppermute | solution.py:44
  22.8 0.7 copy-start.5
  23.5 155.0 %all-gather.6.cloned.1.call-start = ((), (), s32[]{:S(2)}) async-start(), calls=%async_computation.2 | async-start | bytes 2228224 | tf_op jit(solution)/shard_map/all_gather | solution.py:56
  24.3 3.3 %collective-permute-start.1 = (bf16[2,6,256]{2,1,0:T(8,128)(2,1)S(1)}, bf16[2,6,256]{2,1,0:T(8,128)(2,1)S(1)}, u32[]{:S(2)}, u32[]{:S(2)}) collective-permute-start(bf16[2,6,256]{2,1,0:T(8,128)(2,1)S(1)} %pad_maximum_fusion.1), channel_id=1, source_target_pairs={{0,32},{32,64},{64,96},{96,128},{128,160},{160,192},{192,224},{224... | collective-permute-start | bytes 18440 | tf_op jit(solution)/shard_map/ppermute | solution.py:13
  30.5 244.7 %reduce-scatter.2.cloned.1.call-start = ((), (), s32[]{:S(2)}) async-start(), calls=%async_computation.1 | async-start | bytes 4456448 | tf_op jit(solution)/shard_map/reduce_scatter | solution.py:54
  130.2 2.0 copy-start.1
  135.4 139.8 %copy-start.4 = (bf16[256,256]{1,0:T(8,128)(2,1)S(1)}, bf16[256,256]{1,0:T(8,128)(2,1)}, u32[]{:S(2)}) copy-start(bf16[256,256]{1,0:T(8,128)(2,1)} %param.6) | copy-start | bytes 393220
  135.4 169.3 %copy-start.2 = (bf16[256,256]{1,0:T(8,128)(2,1)S(1)}, bf16[256,256]{1,0:T(8,128)(2,1)}, u32[]{:S(2)}) copy-start(bf16[256,256]{1,0:T(8,128)(2,1)} %param.7) | copy-start | bytes 393220
  135.5 170.2 %copy-start.3 = (bf16[256,256]{1,0:T(8,128)(2,1)S(1)}, bf16[256,256]{1,0:T(8,128)(2,1)}, u32[]{:S(2)}) copy-start(bf16[256,256]{1,0:T(8,128)(2,1)} %param.8) | copy-start | bytes 393220
  277.1 27.7 %collective-permute-start.2 = (f32[6,256]{1,0:T(8,128)S(1)}, f32[6,256]{1,0:T(8,128)S(1)}, u32[]{:S(2)}, u32[]{:S(2)}) collective-permute-start(f32[6,256]{1,0:T(8,128)S(1)} %slice.158), channel_id=1, source_target_pairs={{32,0},{64,32},{96,64},{128,96},{160,128},{192,160},{224,192},{256... | collective-permute-start | bytes 18440 | tf_op jit(solution)/shard_map/ppermute | solution.py:13
Sparse Core Ops, SparseCore 0:
  23.6 94.1 all-gather.7
  121.4 57.0 all-gather.5
  182.7 92.4 reduce-scatter.1
